TPU v7x, 128 devices: a whole 4x4x4 slice. The times are simulated.
128 devices in a mesh: nodes: 16 (over x, z), cols: 8 (over y, core).
Axes of the slice: x: 4, y: 4, z: 4, core: 2. Of those that a mesh axis runs over, the one named last changes fastest.
Arguments:
- node_feats: bfloat16 [32768, 256], P(('nodes', 'cols')), may hold values from -6 to 6
- tile_row: int32 [16, 2816], P('nodes', 'cols'), may hold values from 0 to 15, as said below
- tile_col: int32 [16, 2816], P('nodes', 'cols'), may hold values from 0 to 31
- tile_bits: int32 [16, 2816, 16, 128], P('nodes', 'cols'), may hold values from 0 to 255, as said below
- w_self: bfloat16 [256, 256], replicated, may hold values from -0.375 to 0.375
- w_neigh: bfloat16 [256, 256], replicated, may hold values from -1.5 to 1.5
- bias: float32 [256], replicated, may hold values from -3 to 3
- cotangent: bfloat16 [32768, 256], P(('nodes', 'cols')), may hold values from -6 to 6
Outputs:
- layer_out: bfloat16 [32768, 256], P(('nodes', 'cols'))
- feat_grad: bfloat16 [32768, 256], P(('nodes', 'cols'))
- self_grad: float32 [256, 256], replicated
- neigh_grad: float32 [256, 256], replicated
- bias_grad: float32 [256], replicated
Inputs may be any that keep to these rules, and one draw needn't show every extreme that they name: `tile_row`: destination row block of a tile within its nodes group; in every nodes group at least one block carries no tile. `tile_col`: source row block of a tile within its cols index; a block may carry several tiles. `tile_bits`: bit j of word (w, a) of a tile is its edge from destination row a to source column 8 w + j; bits above the eighth are zero; some destination rows have no edge in any tile.
All inputs are finite; a program needn't handle non-finite values.
Results may differ from a plain program's by a relative error of at most 0.0075.
Values may be sent and summed in bfloat16 or wider, within the bound.
No kernel may reach another device: no remote copies, remote signals or barrier semaphores. Data moves between devices by JAX's collectives and lax.ppermute only.
A program may use at most 64 MiB of HBM per device.

v0:
```python
import math
import jax
import jax.numpy as jnp
from jax import lax
from jax.sharding import PartitionSpec as P


def unpack_tiles(packed):
    shifts = jnp.arange(8, dtype=jnp.int32)
    edge_flags = jnp.right_shift(packed[:, :, None, :], shifts[None, None, :, None]) & 1
    return edge_flags.reshape(packed.shape[0], 128, 128)


def shards(node_feats, tile_row, tile_col, tile_bits, w_self, w_neigh, bias, cotangent):
    rows_dev = node_feats.shape[0]
    width_in = node_feats.shape[1]
    node_count = lax.axis_size("nodes")
    col_count = lax.axis_size("cols")
    per_dev = rows_dev // 128
    dest_count = col_count * per_dev
    source_count = node_count * per_dev
    tile_count = tile_row.shape[1]
    tile_group = math.gcd(tile_count, 32)
    group_count = tile_count // tile_group
    rows_here = tile_row[0].reshape(group_count, tile_group)
    cols_here = tile_col[0].reshape(group_count, tile_group)
    packed_here = tile_bits[0].reshape(group_count, tile_group, 16, 128)
    source = lax.all_gather(node_feats, "nodes", axis=0, tiled=True)
    source_blocks = source.reshape(source_count, 128, width_in)

    def forward_step(totals, tile_set):
        summed, degree = totals
        rows_blk, cols_blk, packed_blk = tile_set
        edge_flags = unpack_tiles(packed_blk)
        bits_blk = edge_flags.astype(jnp.bfloat16)
        picked = source_blocks[cols_blk]
        products = jnp.einsum("tba,tbf->taf", bits_blk, picked, preferred_element_type=jnp.float32)
        summed = summed.at[rows_blk].add(products)
        degree = degree.at[rows_blk].add(jnp.sum(edge_flags, axis=1).astype(jnp.float32))
        return ((summed, degree), None)

    initial = (
        jnp.zeros((dest_count, 128, width_in), jnp.float32),
        jnp.zeros((dest_count, 128), jnp.float32),
    )
    (partial_sum, degree_part), _ = lax.scan(
        forward_step, initial, (rows_here, cols_here, packed_here)
    )
    summed, degree = (
        lax.psum_scatter(
            partial_sum.reshape(dest_count * 128, width_in), "cols", scatter_dimension=0, tiled=True
        ),
        lax.psum_scatter(
            degree_part.reshape(dest_count * 128), "cols", scatter_dimension=0, tiled=True
        ),
    )
    degree = jnp.maximum(degree, 1.0)
    neigh_mean = (summed / degree[:, None]).astype(jnp.bfloat16)
    preact = (
        jnp.dot(node_feats, w_self, preferred_element_type=jnp.float32)
        + jnp.dot(neigh_mean, w_neigh, preferred_element_type=jnp.float32)
        + bias
    )
    sigmoid_pre = jax.nn.sigmoid(preact)
    layer_out = (preact * sigmoid_pre).astype(jnp.bfloat16)
    pre_grad = (
        cotangent.astype(jnp.float32) * sigmoid_pre * (1.0 + preact * (1.0 - sigmoid_pre))
    ).astype(jnp.bfloat16)
    self_term = jnp.dot(node_feats.T, pre_grad, preferred_element_type=jnp.float32)
    neigh_term = jnp.dot(neigh_mean.T, pre_grad, preferred_element_type=jnp.float32)
    bias_term = jnp.sum(pre_grad.astype(jnp.float32), axis=0)
    self_grad, neigh_grad, bias_grad = lax.psum(
        (self_term, neigh_term, bias_term), ("nodes", "cols")
    )
    mean_grad = (
        jnp.dot(pre_grad, w_neigh.T, preferred_element_type=jnp.float32) / degree[:, None]
    ).astype(jnp.bfloat16)
    dest_grad = lax.all_gather(mean_grad, "cols", axis=0, tiled=True)
    grad_blocks = dest_grad.reshape(dest_count, 128, width_in)

    def backward_step(src_grad, tile_set):
        rows_blk, cols_blk, packed_blk = tile_set
        bits_blk = unpack_tiles(packed_blk).astype(jnp.bfloat16)
        picked = grad_blocks[rows_blk]
        products = jnp.einsum("tba,taf->tbf", bits_blk, picked, preferred_element_type=jnp.float32)
        return (src_grad.at[cols_blk].add(products), None)

    src_total, _ = lax.scan(
        backward_step,
        jnp.zeros((source_count, 128, width_in), jnp.float32),
        (rows_here, cols_here, packed_here),
    )
    src_total = src_total.reshape(source_count * 128, width_in)
    src_grad = lax.psum_scatter(src_total, "nodes", scatter_dimension=0, tiled=True)
    feat_grad = (jnp.dot(pre_grad, w_self.T, preferred_element_type=jnp.float32) + src_grad).astype(
        jnp.bfloat16
    )
    return (layer_out, feat_grad, self_grad, neigh_grad, bias_grad)


def solution(mesh):
    return jax.shard_map(
        shards,
        mesh=mesh,
        in_specs=(
            P(("nodes", "cols"), None),
            P("nodes", "cols"),
            P("nodes", "cols"),
            P("nodes", "cols", None, None),
            P(),
            P(),
            P(),
            P(("nodes", "cols"), None),
        ),
        out_specs=(P(("nodes", "cols"), None), P(("nodes", "cols"), None), P(), P(), P()),
        check_vma=False,
    )
```

profile of v0, /device:TPU:0, one launch (start us, length us, event | category | flops | bytes accessed | tf_op | source)
XLA Modules:
  0.0 557.2 jit_solution(13627646105467495376)
XLA Ops:
  9.5 48.4 %all-gather.3.cloned.1.call-done = bf16[4096,256]{1,0:T(8,128)(2,1)} async-done(((bf16[256,256]{1,0:T(8,128)(2,1)}), bf16[4096,256]{1,0:T(8,128)(2,1)}) %all-gather.3.cloned.1.call-update) | async-done | bytes 2097168 | tf_op jit(solution)/shard_map/all_gather | solution.py:28
  58.1 182.1 %while.22 = (s32[]{:T(128)}, f32[16,128,256]{2,1,0:T(8,128)S(1)}, f32[16,128]{1,0:T(8,128)S(1)}, s32[11,32]{1,0:T(8,128)S(1)}, s32[11,32,16,128]{3,2,1,0:T(8,128...) while((s32[]{:T(128)}, f32[16,128,256]{2,1,0:T(8,128)S(1)}, ...), condition=%wide.region_4.5_spmd, body=%wide.region_0.4_spmd.sunk | while | flops 272635072 | bytes 24165348 | solution.py:46
  67.2 6.5 %scatter_fusion = f32[16,128,256]{2,1,0:T(8,128)S(1)} fusion(f32[16,128,256]{2,1,0:T(8,128)S(1)} %get-tuple-element.232, s32[32]{0:T(128)S(1)} %get-tuple-element.213, f32[32,128,256]{2,1,0:T(8,128)} %fusion.56), kind=kCustom, calls=%fused_computation.2.clone.1 | custom fusion | flops 1048576 | bytes 12583040 | tf_op jit(solution)/shard_map/while/body/eval_jaxpr/scatter-add | solution.py:38
  83.8 6.5 %scatter_fusion = f32[16,128,256]{2,1,0:T(8,128)S(1)} fusion(f32[16,128,256]{2,1,0:T(8,128)S(1)} %get-tuple-element.232, s32[32]{0:T(128)S(1)} %get-tuple-element.213, f32[32,128,256]{2,1,0:T(8,128)} %fusion.56), kind=kCustom, calls=%fused_computation.2.clone.1 | custom fusion | flops 1048576 | bytes 12583040 | tf_op jit(solution)/shard_map/while/body/eval_jaxpr/scatter-add | solution.py:38
  100.4 6.5 %scatter_fusion = f32[16,128,256]{2,1,0:T(8,128)S(1)} fusion(f32[16,128,256]{2,1,0:T(8,128)S(1)} %get-tuple-element.232, s32[32]{0:T(128)S(1)} %get-tuple-element.213, f32[32,128,256]{2,1,0:T(8,128)} %fusion.56), kind=kCustom, calls=%fused_computation.2.clone.1 | custom fusion | flops 1048576 | bytes 12583040 | tf_op jit(solution)/shard_map/while/body/eval_jaxpr/scatter-add | solution.py:38
  112.5 4.4 fusion.56
  116.9 6.5 %scatter_fusion = f32[16,128,256]{2,1,0:T(8,128)S(1)} fusion(f32[16,128,256]{2,1,0:T(8,128)S(1)} %get-tuple-element.232, s32[32]{0:T(128)S(1)} %get-tuple-element.213, f32[32,128,256]{2,1,0:T(8,128)} %fusion.56), kind=kCustom, calls=%fused_computation.2.clone.1 | custom fusion | flops 1048576 | bytes 12583040 | tf_op jit(solution)/shard_map/while/body/eval_jaxpr/scatter-add | solution.py:38
  133.5 6.5 %scatter_fusion = f32[16,128,256]{2,1,0:T(8,128)S(1)} fusion(f32[16,128,256]{2,1,0:T(8,128)S(1)} %get-tuple-element.232, s32[32]{0:T(128)S(1)} %get-tuple-element.213, f32[32,128,256]{2,1,0:T(8,128)} %fusion.56), kind=kCustom, calls=%fused_computation.2.clone.1 | custom fusion | flops 1048576 | bytes 12583040 | tf_op jit(solution)/shard_map/while/body/eval_jaxpr/scatter-add | solution.py:38
  150.0 6.5 %scatter_fusion = f32[16,128,256]{2,1,0:T(8,128)S(1)} fusion(f32[16,128,256]{2,1,0:T(8,128)S(1)} %get-tuple-element.232, s32[32]{0:T(128)S(1)} %get-tuple-element.213, f32[32,128,256]{2,1,0:T(8,128)} %fusion.56), kind=kCustom, calls=%fused_computation.2.clone.1 | custom fusion | flops 1048576 | bytes 12583040 | tf_op jit(solution)/shard_map/while/body/eval_jaxpr/scatter-add | solution.py:38
  166.6 6.5 %scatter_fusion = f32[16,128,256]{2,1,0:T(8,128)S(1)} fusion(f32[16,128,256]{2,1,0:T(8,128)S(1)} %get-tuple-element.232, s32[32]{0:T(128)S(1)} %get-tuple-element.213, f32[32,128,256]{2,1,0:T(8,128)} %fusion.56), kind=kCustom, calls=%fused_computation.2.clone.1 | custom fusion | flops 1048576 | bytes 12583040 | tf_op jit(solution)/shard_map/while/body/eval_jaxpr/scatter-add | solution.py:38
  178.7 4.4 fusion.56
  183.1 6.5 %scatter_fusion = f32[16,128,256]{2,1,0:T(8,128)S(1)} fusion(f32[16,128,256]{2,1,0:T(8,128)S(1)} %get-tuple-element.232, s32[32]{0:T(128)S(1)} %get-tuple-element.213, f32[32,128,256]{2,1,0:T(8,128)} %fusion.56), kind=kCustom, calls=%fused_computation.2.clone.1 | custom fusion | flops 1048576 | bytes 12583040 | tf_op jit(solution)/shard_map/while/body/eval_jaxpr/scatter-add | solution.py:38
  199.7 6.5 %scatter_fusion = f32[16,128,256]{2,1,0:T(8,128)S(1)} fusion(f32[16,128,256]{2,1,0:T(8,128)S(1)} %get-tuple-element.232, s32[32]{0:T(128)S(1)} %get-tuple-element.213, f32[32,128,256]{2,1,0:T(8,128)} %fusion.56), kind=kCustom, calls=%fused_computation.2.clone.1 | custom fusion | flops 1048576 | bytes 12583040 | tf_op jit(solution)/shard_map/while/body/eval_jaxpr/scatter-add | solution.py:38
  216.2 6.5 %scatter_fusion = f32[16,128,256]{2,1,0:T(8,128)S(1)} fusion(f32[16,128,256]{2,1,0:T(8,128)S(1)} %get-tuple-element.232, s32[32]{0:T(128)S(1)} %get-tuple-element.213, f32[32,128,256]{2,1,0:T(8,128)} %fusion.56), kind=kCustom, calls=%fused_computation.2.clone.1 | custom fusion | flops 1048576 | bytes 12583040 | tf_op jit(solution)/shard_map/while/body/eval_jaxpr/scatter-add | solution.py:38
  232.8 6.5 %scatter_fusion = f32[16,128,256]{2,1,0:T(8,128)S(1)} fusion(f32[16,128,256]{2,1,0:T(8,128)S(1)} %get-tuple-element.232, s32[32]{0:T(128)S(1)} %get-tuple-element.213, f32[32,128,256]{2,1,0:T(8,128)} %fusion.56), kind=kCustom, calls=%fused_computation.2.clone.1 | custom fusion | flops 1048576 | bytes 12583040 | tf_op jit(solution)/shard_map/while/body/eval_jaxpr/scatter-add | solution.py:38
  243.1 13.7 %all-reduce = f32[2048]{0:T(1024)S(1)} all-reduce(f32[2048]{0:T(1024)S(1)} %bitcast.96), channel_id=3, replica_groups=mesh['nodes'=16,'cols'=8] {'cols'}, use_global_device_ids=true, to_apply=%region_6.7.clone | all-reduce | flops 2048 | bytes 16384
  256.9 17.8 %reduce-scatter.3.cloned.1.call-done = f32[256,256]{1,0:T(8,128)} async-done(((f32[2048,256]{1,0:T(8,128)}), f32[256,256]{1,0:T(8,128)}) %reduce-scatter.3.cloned.1.call-update) | async-done | bytes 262160 | tf_op jit(solution)/shard_map/reduce_scatter | solution.py:50
  280.3 20.2 %all-gather.5.cloned.1.call-done = bf16[2048,256]{1,0:T(8,128)(2,1)} async-done(((bf16[256,256]{1,0:T(8,128)(2,1)}), bf16[2048,256]{1,0:T(8,128)(2,1)}) %all-gather.5.cloned.1.call-update) | async-done | bytes 1048592 | tf_op jit(solution)/shard_map/all_gather | solution.py:78
  302.9 166.3 %while.23 = (s32[]{:T(128)}, f32[32,128,256]{2,1,0:T(8,128)}, s32[11,32]{1,0:T(8,128)}, s32[11,32,16,128]{3,2,1,0:T(8,128)}, s32[11,32]{1,0:T(8,128)}, /*index=5*/bf16[16,128,256]{2,1,0:T(8,128)(2,1)S(1)}, s32[]{:T(128)}) while((s32[]{:T(128)}, f32[32,128,256]{2,1,0:T(8,128)}, s32[11,32]{1,0:T(8,128)}, s32[11,32,16,128]{3,2,1,0:T(8,128)}, ...), condition=%wide.region_9.10_spmd, body=%wide.region_7.9_spmd.sunk | while | flops 271058112 | bytes 23862236 | solution.py:88
  308.1 9.9 %scatter_fusion.1 = f32[32,128,256]{2,1,0:T(8,128)} fusion(f32[32,128,256]{2,1,0:T(8,128)} %get-tuple-element.255, s32[32]{0:T(128)S(1)} %get-tuple-element.221, f32[32,128,256]{2,1,0:T(8,128)} %fusion.60), kind=kCustom, calls=%fused_computation.4.clone.1 | custom fusion | flops 1048576 | bytes 12583040 | tf_op jit(solution)/shard_map/while/body/eval_jaxpr/scatter-add | solution.py:86
  323.2 9.9 %scatter_fusion.1 = f32[32,128,256]{2,1,0:T(8,128)} fusion(f32[32,128,256]{2,1,0:T(8,128)} %get-tuple-element.255, s32[32]{0:T(128)S(1)} %get-tuple-element.221, f32[32,128,256]{2,1,0:T(8,128)} %fusion.60), kind=kCustom, calls=%fused_computation.4.clone.1 | custom fusion | flops 1048576 | bytes 12583040 | tf_op jit(solution)/shard_map/while/body/eval_jaxpr/scatter-add | solution.py:86
  338.3 9.9 %scatter_fusion.1 = f32[32,128,256]{2,1,0:T(8,128)} fusion(f32[32,128,256]{2,1,0:T(8,128)} %get-tuple-element.255, s32[32]{0:T(128)S(1)} %get-tuple-element.221, f32[32,128,256]{2,1,0:T(8,128)} %fusion.60), kind=kCustom, calls=%fused_computation.4.clone.1 | custom fusion | flops 1048576 | bytes 12583040 | tf_op jit(solution)/shard_map/while/body/eval_jaxpr/scatter-add | solution.py:86
  353.3 9.9 %scatter_fusion.1 = f32[32,128,256]{2,1,0:T(8,128)} fusion(f32[32,128,256]{2,1,0:T(8,128)} %get-tuple-element.255, s32[32]{0:T(128)S(1)} %get-tuple-element.221, f32[32,128,256]{2,1,0:T(8,128)} %fusion.60), kind=kCustom, calls=%fused_computation.4.clone.1 | custom fusion | flops 1048576 | bytes 12583040 | tf_op jit(solution)/shard_map/while/body/eval_jaxpr/scatter-add | solution.py:86
  368.4 9.9 %scatter_fusion.1 = f32[32,128,256]{2,1,0:T(8,128)} fusion(f32[32,128,256]{2,1,0:T(8,128)} %get-tuple-element.255, s32[32]{0:T(128)S(1)} %get-tuple-element.221, f32[32,128,256]{2,1,0:T(8,128)} %fusion.60), kind=kCustom, calls=%fused_computation.4.clone.1 | custom fusion | flops 1048576 | bytes 12583040 | tf_op jit(solution)/shard_map/while/body/eval_jaxpr/scatter-add | solution.py:86
  383.5 10.0 %scatter_fusion.1 = f32[32,128,256]{2,1,0:T(8,128)} fusion(f32[32,128,256]{2,1,0:T(8,128)} %get-tuple-element.255, s32[32]{0:T(128)S(1)} %get-tuple-element.221, f32[32,128,256]{2,1,0:T(8,128)} %fusion.60), kind=kCustom, calls=%fused_computation.4.clone.1 | custom fusion | flops 1048576 | bytes 12583040 | tf_op jit(solution)/shard_map/while/body/eval_jaxpr/scatter-add | solution.py:86
  398.7 10.2 %scatter_fusion.1 = f32[32,128,256]{2,1,0:T(8,128)} fusion(f32[32,128,256]{2,1,0:T(8,128)} %get-tuple-element.255, s32[32]{0:T(128)S(1)} %get-tuple-element.221, f32[32,128,256]{2,1,0:T(8,128)} %fusion.60), kind=kCustom, calls=%fused_computation.4.clone.1 | custom fusion | flops 1048576 | bytes 12583040 | tf_op jit(solution)/shard_map/while/body/eval_jaxpr/scatter-add | solution.py:86
  414.1 9.9 %scatter_fusion.1 = f32[32,128,256]{2,1,0:T(8,128)} fusion(f32[32,128,256]{2,1,0:T(8,128)} %get-tuple-element.255, s32[32]{0:T(128)S(1)} %get-tuple-element.221, f32[32,128,256]{2,1,0:T(8,128)} %fusion.60), kind=kCustom, calls=%fused_computation.4.clone.1 | custom fusion | flops 1048576 | bytes 12583040 | tf_op jit(solution)/shard_map/while/body/eval_jaxpr/scatter-add | solution.py:86
  429.1 10.0 %scatter_fusion.1 = f32[32,128,256]{2,1,0:T(8,128)} fusion(f32[32,128,256]{2,1,0:T(8,128)} %get-tuple-element.255, s32[32]{0:T(128)S(1)} %get-tuple-element.221, f32[32,128,256]{2,1,0:T(8,128)} %fusion.60), kind=kCustom, calls=%fused_computation.4.clone.1 | custom fusion | flops 1048576 | bytes 12583040 | tf_op jit(solution)/shard_map/while/body/eval_jaxpr/scatter-add | solution.py:86
  444.3 9.9 %scatter_fusion.1 = f32[32,128,256]{2,1,0:T(8,128)} fusion(f32[32,128,256]{2,1,0:T(8,128)} %get-tuple-element.255, s32[32]{0:T(128)S(1)} %get-tuple-element.221, f32[32,128,256]{2,1,0:T(8,128)} %fusion.60), kind=kCustom, calls=%fused_computation.4.clone.1 | custom fusion | flops 1048576 | bytes 12583040 | tf_op jit(solution)/shard_map/while/body/eval_jaxpr/scatter-add | solution.py:86
  459.4 9.8 %scatter_fusion.1 = f32[32,128,256]{2,1,0:T(8,128)} fusion(f32[32,128,256]{2,1,0:T(8,128)} %get-tuple-element.255, s32[32]{0:T(128)S(1)} %get-tuple-element.221, f32[32,128,256]{2,1,0:T(8,128)} %fusion.60), kind=kCustom, calls=%fused_computation.4.clone.1 | custom fusion | flops 1048576 | bytes 12583040 | tf_op jit(solution)/shard_map/while/body/eval_jaxpr/scatter-add | solution.py:86
  469.8 66.2 %psum.23 = f32[256]{0:T(256)} all-reduce(f32[256]{0:T(256)S(1)} %copy-done.7), channel_id=1, replica_groups=mesh['nodes'=16,'cols'=8] {'nodes','cols'}, use_global_device_ids=true, to_apply=%region_14.15 | all-reduce | flops 256 | bytes 2048 | tf_op jit(solution)/shard_map/psum | solution.py:72
  537.9 9.3 %reduce-scatter.5.cloned.1.call-done = f32[256,256]{1,0:T(8,128)} async-done(((f32[4096,256]{1,0:T(8,128)}), f32[256,256]{1,0:T(8,128)}) %reduce-scatter.5.cloned.1.call-update) | async-done | bytes 262160 | tf_op jit(solution)/shard_map/reduce_scatter | solution.py:94
  (226 shorter events, 177.1 us)
Async XLA Ops:
  7.2 267.5 %copy-start = (bf16[256,256]{1,0:T(8,128)(2,1)S(1)}, bf16[256,256]{1,0:T(8,128)(2,1)}, u32[]{:S(2)}) copy-start(bf16[256,256]{1,0:T(8,128)(2,1)} %param.17) | copy-start | bytes 393220
  7.2 50.7 %all-gather.3.cloned.1.call-start = ((), (), s32[]{:S(2)}) async-start(), calls=%async_computation.2 | async-start | bytes 2228224 | tf_op jit(solution)/shard_map/all_gather | solution.py:28
  7.9 266.8 %reduce-scatter.3.cloned.1.call-start = ((), (), s32[]{:S(2)}) async-start(), calls=%async_computation.3 | async-start | bytes 2359296 | tf_op jit(solution)/shard_map/reduce_scatter | solution.py:50
  240.2 1.4 copy-start.1
  240.2 2.0 copy-start.5
  240.2 2.0 copy-start.6
  240.3 1.4 copy-start.11
  240.3 2.6 copy-start.3
  240.3 2.6 copy-start.4
  240.3 34.4 %copy-start.9 = (bf16[256,256]{1,0:T(8,128)(2,1)S(1)}, bf16[256,256]{1,0:T(8,128)(2,1)}, u32[]{:S(2)}) copy-start(bf16[256,256]{1,0:T(8,128)(2,1)} %param.19) | copy-start | bytes 393220
  240.3 34.4 %copy-start.10 = (f32[256]{0:T(256)S(1)}, f32[256]{0:T(256)}, u32[]{:S(2)}) copy-start(f32[256]{0:T(256)} %param.18) | copy-start | bytes 3076
  241.6 58.9 %all-gather.5.cloned.1.call-start = ((), (), s32[]{:S(2)}) async-start(), calls=%async_computation.4 | async-start | bytes 1179648 | tf_op jit(solution)/shard_map/all_gather | solution.py:78
  274.7 4.5 copy-start.8
  278.2 257.9 %all-reduce.4.cloned.1.call-start = ((), (), s32[]{:S(2)}) async-start(), calls=%async_computation.6 | async-start | bytes 1048576 | tf_op jit(solution)/shard_map/psum | solution.py:72
  280.2 267.0 %reduce-scatter.5.cloned.1.call-start = ((), (), s32[]{:S(2)}) async-start(), calls=%async_computation.5 | async-start | bytes 4456448 | tf_op jit(solution)/shard_map/reduce_scatter | solution.py:94
  300.5 2.4 copy-start.2
  469.2 0.7 copy-start.7
Sparse Core Ops, SparseCore 0:
  10.2 47.7 all-gather.2
  241.7 32.9 reduce-scatter.2
  278.3 22.1 all-gather.4
  305.8 144.6 all-reduce.3
  469.3 77.8 reduce-scatter.4
where the time goes:
time: 560 us; the launch traced here: 557 us
  other arithmetic  200 us (36%)
  waiting for transfers between devices  96.4 us (17%)
  matrix products  85.6 us (15%)
  blocking collectives  80 us (14%)
  local copies, waits for them, and re-layouts  79.4 us (14%)
  between operations  14.6 us (3%)
    scatter-add x11, other arithmetic, backward_step(): return (src_grad.at[cols_blk].add(products), None)  109 us
    scatter-add x11, other arithmetic, forward_step(): summed = summed.at[rows_blk].add(products)  71.1 us
    psum x1, blocking collectives, shards(): lax.psum((self_term, neigh_term, bias_term), ('nodes', 'cols'))  66.2 us
    all_gather x1, waiting for transfers between devices, shards(): source = lax.all_gather(node_feats, 'nodes', axis=0, tiled=True)  48.4 us
    dot_general x11, matrix products, forward_step(): jnp.einsum('tba,tbf->taf', bits_blk, picked, preferred_element_type=jnp.f...  48.1 us
    gather x11, local copies, waits for them, and re-layouts, forward_step(): picked = source_blocks[cols_blk]  39.8 us
    dot_general x11, matrix products, backward_step(): jnp.einsum('tba,taf->tbf', bits_blk, picked, preferred_element_type=jnp.f...  30.1 us
    shift_right_arithmetic x66, local copies, waits for them, and re-layouts, unpack_tiles(): jnp.right_shift(packed[:, :, None, :], shifts[None, None, :, None]) & 1  23.4 us
  transfers between devices with their start and end apart: 5, of which 4 were waited for; matrix products, arithmetic and copies ran while one was open for 31% of the time, Pallas kernels for 0%

commit v1 on v0

--- a/solution.py
+++ b/solution.py
@@ -3,6 +3,11 @@
 import jax.numpy as jnp
 from jax import lax
 from jax.sharding import PartitionSpec as P
+
+
+def axis_by_axis(value, inner_axis, outer_axis):
+    partial = lax.psum(value, inner_axis)
+    return lax.psum(partial, outer_axis)
 
 
 def unpack_tiles(packed):
@@ -69,8 +74,8 @@
     self_term = jnp.dot(node_feats.T, pre_grad, preferred_element_type=jnp.float32)
     neigh_term = jnp.dot(neigh_mean.T, pre_grad, preferred_element_type=jnp.float32)
     bias_term = jnp.sum(pre_grad.astype(jnp.float32), axis=0)
-    self_grad, neigh_grad, bias_grad = lax.psum(
-        (self_term, neigh_term, bias_term), ("nodes", "cols")
+    self_grad, neigh_grad, bias_grad = axis_by_axis(
+        (self_term, neigh_term, bias_term), "nodes", "cols"
     )
     mean_grad = (
         jnp.dot(pre_grad, w_neigh.T, preferred_element_type=jnp.float32) / degree[:, None]

time: 560 us -> 648 us (1.16)
  waiting for transfers between devices: 96.4 us -> 196 us
  blocking collectives: 80 us -> 68.3 us
    psum x1 -> x2, waiting for transfers between devices: 0.01 us -> 83.3 us  [the longest x1 83.3 us: axis_by_axis(): partial = lax.psum(value, inner_axis)]
    psum x1 -> x2, blocking collectives: 66.2 us -> 54.6 us  [the longest x1 40.9 us: axis_by_axis(): partial = lax.psum(value, inner_axis)]
    reduce_scatter x1, waiting for transfers between devices: 9.32 us -> 20.8 us  [shards(): lax.psum_scatter(src_total, 'nodes', scatter_dimension=0, tiled=True)]
  transfers between devices with their start and end apart: 5 -> 6, of which waited for: 4 -> 5; matrix products, arithmetic and copies ran while one was open for 31% -> 27% of each run, Pallas kernels for 0% -> 0%
where the time goes in v1:
time: 648 us; the launch traced here: 645 us
  other arithmetic  200 us (31%)
  waiting for transfers between devices  196 us (30%)
  matrix products  85.6 us (13%)
  local copies, waits for them, and re-layouts  79.4 us (12%)
  blocking collectives  68.3 us (11%)
  between operations  14.9 us (2%)
    scatter-add x11, other arithmetic, backward_step(): return (src_grad.at[cols_blk].add(products), None)  109 us
    psum x1, waiting for transfers between devices, axis_by_axis(): partial = lax.psum(value, inner_axis)  83.3 us
    scatter-add x11, other arithmetic, forward_step(): summed = summed.at[rows_blk].add(products)  71.1 us
    all_gather x1, waiting for transfers between devices, shards(): source = lax.all_gather(node_feats, 'nodes', axis=0, tiled=True)  48.4 us
    dot_general x11, matrix products, forward_step(): jnp.einsum('tba,tbf->taf', bits_blk, picked, preferred_element_type=jnp.f...  48.1 us
    psum x1, blocking collectives, axis_by_axis(): partial = lax.psum(value, inner_axis)  40.9 us
    gather x11, local copies, waits for them, and re-layouts, forward_step(): picked = source_blocks[cols_blk]  39.8 us
    dot_general x11, matrix products, backward_step(): jnp.einsum('tba,taf->tbf', bits_blk, picked, preferred_element_type=jnp.f...  30.1 us
  transfers between devices with their start and end apart: 6, of which 5 were waited for; matrix products, arithmetic and copies ran while one was open for 27% of the time, Pallas kernels for 0%

profile of v1, /device:TPU:0, one launch (start us, length us, event | category | flops | bytes accessed | tf_op | source)
XLA Modules:
  0.0 645.3 jit_solution(16224214653045145665)
XLA Ops:
  9.5 48.4 %all-gather.3.cloned.1.call-done = bf16[4096,256]{1,0:T(8,128)(2,1)} async-done(((bf16[256,256]{1,0:T(8,128)(2,1)}), bf16[4096,256]{1,0:T(8,128)(2,1)}) %all-gather.3.cloned.1.call-update) | async-done | bytes 2097168 | tf_op jit(solution)/shard_map/all_gather | solution.py:33
  58.1 182.1 %while.22 = (s32[]{:T(128)}, f32[16,128,256]{2,1,0:T(8,128)S(1)}, f32[16,128]{1,0:T(8,128)S(1)}, s32[11,32]{1,0:T(8,128)S(1)}, s32[11,32,16,128]{3,2,1,0:T(8,128...) while((s32[]{:T(128)}, f32[16,128,256]{2,1,0:T(8,128)S(1)}, ...), condition=%wide.region_4.5_spmd, body=%wide.region_0.4_spmd.sunk | while | flops 272635072 | bytes 24165348 | solution.py:51
  67.2 6.5 %scatter_fusion = f32[16,128,256]{2,1,0:T(8,128)S(1)} fusion(f32[16,128,256]{2,1,0:T(8,128)S(1)} %get-tuple-element.234, s32[32]{0:T(128)S(1)} %get-tuple-element.215, f32[32,128,256]{2,1,0:T(8,128)} %fusion.56), kind=kCustom, calls=%fused_computation.2.clone.1 | custom fusion | flops 1048576 | bytes 12583040 | tf_op jit(solution)/shard_map/while/body/eval_jaxpr/scatter-add | solution.py:43
  83.8 6.5 %scatter_fusion = f32[16,128,256]{2,1,0:T(8,128)S(1)} fusion(f32[16,128,256]{2,1,0:T(8,128)S(1)} %get-tuple-element.234, s32[32]{0:T(128)S(1)} %get-tuple-element.215, f32[32,128,256]{2,1,0:T(8,128)} %fusion.56), kind=kCustom, calls=%fused_computation.2.clone.1 | custom fusion | flops 1048576 | bytes 12583040 | tf_op jit(solution)/shard_map/while/body/eval_jaxpr/scatter-add | solution.py:43
  100.4 6.5 %scatter_fusion = f32[16,128,256]{2,1,0:T(8,128)S(1)} fusion(f32[16,128,256]{2,1,0:T(8,128)S(1)} %get-tuple-element.234, s32[32]{0:T(128)S(1)} %get-tuple-element.215, f32[32,128,256]{2,1,0:T(8,128)} %fusion.56), kind=kCustom, calls=%fused_computation.2.clone.1 | custom fusion | flops 1048576 | bytes 12583040 | tf_op jit(solution)/shard_map/while/body/eval_jaxpr/scatter-add | solution.py:43
  116.9 6.5 %scatter_fusion = f32[16,128,256]{2,1,0:T(8,128)S(1)} fusion(f32[16,128,256]{2,1,0:T(8,128)S(1)} %get-tuple-element.234, s32[32]{0:T(128)S(1)} %get-tuple-element.215, f32[32,128,256]{2,1,0:T(8,128)} %fusion.56), kind=kCustom, calls=%fused_computation.2.clone.1 | custom fusion | flops 1048576 | bytes 12583040 | tf_op jit(solution)/shard_map/while/body/eval_jaxpr/scatter-add | solution.py:43
  133.5 6.5 %scatter_fusion = f32[16,128,256]{2,1,0:T(8,128)S(1)} fusion(f32[16,128,256]{2,1,0:T(8,128)S(1)} %get-tuple-element.234, s32[32]{0:T(128)S(1)} %get-tuple-element.215, f32[32,128,256]{2,1,0:T(8,128)} %fusion.56), kind=kCustom, calls=%fused_computation.2.clone.1 | custom fusion | flops 1048576 | bytes 12583040 | tf_op jit(solution)/shard_map/while/body/eval_jaxpr/scatter-add | solution.py:43
  150.0 6.5 %scatter_fusion = f32[16,128,256]{2,1,0:T(8,128)S(1)} fusion(f32[16,128,256]{2,1,0:T(8,128)S(1)} %get-tuple-element.234, s32[32]{0:T(128)S(1)} %get-tuple-element.215, f32[32,128,256]{2,1,0:T(8,128)} %fusion.56), kind=kCustom, calls=%fused_computation.2.clone.1 | custom fusion | flops 1048576 | bytes 12583040 | tf_op jit(solution)/shard_map/while/body/eval_jaxpr/scatter-add | solution.py:43
  166.6 6.5 %scatter_fusion = f32[16,128,256]{2,1,0:T(8,128)S(1)} fusion(f32[16,128,256]{2,1,0:T(8,128)S(1)} %get-tuple-element.234, s32[32]{0:T(128)S(1)} %get-tuple-element.215, f32[32,128,256]{2,1,0:T(8,128)} %fusion.56), kind=kCustom, calls=%fused_computation.2.clone.1 | custom fusion | flops 1048576 | bytes 12583040 | tf_op jit(solution)/shard_map/while/body/eval_jaxpr/scatter-add | solution.py:43
  183.1 6.5 %scatter_fusion = f32[16,128,256]{2,1,0:T(8,128)S(1)} fusion(f32[16,128,256]{2,1,0:T(8,128)S(1)} %get-tuple-element.234, s32[32]{0:T(128)S(1)} %get-tuple-element.215, f32[32,128,256]{2,1,0:T(8,128)} %fusion.56), kind=kCustom, calls=%fused_computation.2.clone.1 | custom fusion | flops 1048576 | bytes 12583040 | tf_op jit(solution)/shard_map/while/body/eval_jaxpr/scatter-add | solution.py:43
  199.7 6.5 %scatter_fusion = f32[16,128,256]{2,1,0:T(8,128)S(1)} fusion(f32[16,128,256]{2,1,0:T(8,128)S(1)} %get-tuple-element.234, s32[32]{0:T(128)S(1)} %get-tuple-element.215, f32[32,128,256]{2,1,0:T(8,128)} %fusion.56), kind=kCustom, calls=%fused_computation.2.clone.1 | custom fusion | flops 1048576 | bytes 12583040 | tf_op jit(solution)/shard_map/while/body/eval_jaxpr/scatter-add | solution.py:43
  216.2 6.5 %scatter_fusion = f32[16,128,256]{2,1,0:T(8,128)S(1)} fusion(f32[16,128,256]{2,1,0:T(8,128)S(1)} %get-tuple-element.234, s32[32]{0:T(128)S(1)} %get-tuple-element.215, f32[32,128,256]{2,1,0:T(8,128)} %fusion.56), kind=kCustom, calls=%fused_computation.2.clone.1 | custom fusion | flops 1048576 | bytes 12583040 | tf_op jit(solution)/shard_map/while/body/eval_jaxpr/scatter-add | solution.py:43
  232.8 6.5 %scatter_fusion = f32[16,128,256]{2,1,0:T(8,128)S(1)} fusion(f32[16,128,256]{2,1,0:T(8,128)S(1)} %get-tuple-element.234, s32[32]{0:T(128)S(1)} %get-tuple-element.215, f32[32,128,256]{2,1,0:T(8,128)} %fusion.56), kind=kCustom, calls=%fused_computation.2.clone.1 | custom fusion | flops 1048576 | bytes 12583040 | tf_op jit(solution)/shard_map/while/body/eval_jaxpr/scatter-add | solution.py:43
  243.1 13.7 %all-reduce = f32[2048]{0:T(1024)S(1)} all-reduce(f32[2048]{0:T(1024)S(1)} %bitcast.96), channel_id=3, replica_groups=mesh['nodes'=16,'cols'=8] {'cols'}, use_global_device_ids=true, to_apply=%region_6.7.clone | all-reduce | flops 2048 | bytes 16384
  256.9 17.8 %reduce-scatter.3.cloned.1.call-done = f32[256,256]{1,0:T(8,128)} async-done(((f32[2048,256]{1,0:T(8,128)}), f32[256,256]{1,0:T(8,128)}) %reduce-scatter.3.cloned.1.call-update) | async-done | bytes 262160 | tf_op jit(solution)/shard_map/reduce_scatter | solution.py:55
  280.3 83.3 %all-reduce.6.cloned.1.call-done = (f32[256,256]{0,1:T(8,128)}, f32[256,256]{1,0:T(8,128)}) async-done(((f32[256,256]{0,1:T(8,128)}, f32[256,256]{1,0:T(8,128)}), (f32[256,256]{0,1:T(8,128)}, f32[256,256]{1,0:T(8,128)})) %all-reduce.6.cloned.1.call-update) | async-done | bytes 524304 | tf_op jit(solution)/shard_map/psum | solution.py:9
  363.6 24.9 %all-gather.5.cloned.1.call-done = bf16[2048,256]{1,0:T(8,128)(2,1)} async-done(((bf16[256,256]{1,0:T(8,128)(2,1)}), bf16[2048,256]{1,0:T(8,128)(2,1)}) %all-gather.5.cloned.1.call-update) | async-done | bytes 1048592 | tf_op jit(solution)/shard_map/all_gather | solution.py:83
  390.9 166.1 %while.23 = (s32[]{:T(128)}, f32[32,128,256]{2,1,0:T(8,128)}, s32[11,32]{1,0:T(8,128)}, s32[11,32,16,128]{3,2,1,0:T(8,128)}, s32[11,32]{1,0:T(8,128)}, /*index=5*/bf16[16,128,256]{2,1,0:T(8,128)(2,1)S(1)}, s32[]{:T(128)}) while((s32[]{:T(128)}, f32[32,128,256]{2,1,0:T(8,128)}, s32[11,32]{1,0:T(8,128)}, s32[11,32,16,128]{3,2,1,0:T(8,128)}, ...), condition=%wide.region_9.10_spmd, body=%wide.region_7.9_spmd.sunk | while | flops 271058112 | bytes 23862236 | solution.py:93
  396.1 9.8 %scatter_fusion.1 = f32[32,128,256]{2,1,0:T(8,128)} fusion(f32[32,128,256]{2,1,0:T(8,128)} %get-tuple-element.257, s32[32]{0:T(128)S(1)} %get-tuple-element.223, f32[32,128,256]{2,1,0:T(8,128)} %fusion.60), kind=kCustom, calls=%fused_computation.4.clone.1 | custom fusion | flops 1048576 | bytes 12583040 | tf_op jit(solution)/shard_map/while/body/eval_jaxpr/scatter-add | solution.py:91
  411.2 9.9 %scatter_fusion.1 = f32[32,128,256]{2,1,0:T(8,128)} fusion(f32[32,128,256]{2,1,0:T(8,128)} %get-tuple-element.257, s32[32]{0:T(128)S(1)} %get-tuple-element.223, f32[32,128,256]{2,1,0:T(8,128)} %fusion.60), kind=kCustom, calls=%fused_computation.4.clone.1 | custom fusion | flops 1048576 | bytes 12583040 | tf_op jit(solution)/shard_map/while/body/eval_jaxpr/scatter-add | solution.py:91
  426.3 9.9 %scatter_fusion.1 = f32[32,128,256]{2,1,0:T(8,128)} fusion(f32[32,128,256]{2,1,0:T(8,128)} %get-tuple-element.257, s32[32]{0:T(128)S(1)} %get-tuple-element.223, f32[32,128,256]{2,1,0:T(8,128)} %fusion.60), kind=kCustom, calls=%fused_computation.4.clone.1 | custom fusion | flops 1048576 | bytes 12583040 | tf_op jit(solution)/shard_map/while/body/eval_jaxpr/scatter-add | solution.py:91
  441.3 9.9 %scatter_fusion.1 = f32[32,128,256]{2,1,0:T(8,128)} fusion(f32[32,128,256]{2,1,0:T(8,128)} %get-tuple-element.257, s32[32]{0:T(128)S(1)} %get-tuple-element.223, f32[32,128,256]{2,1,0:T(8,128)} %fusion.60), kind=kCustom, calls=%fused_computation.4.clone.1 | custom fusion | flops 1048576 | bytes 12583040 | tf_op jit(solution)/shard_map/while/body/eval_jaxpr/scatter-add | solution.py:91
  456.4 9.9 %scatter_fusion.1 = f32[32,128,256]{2,1,0:T(8,128)} fusion(f32[32,128,256]{2,1,0:T(8,128)} %get-tuple-element.257, s32[32]{0:T(128)S(1)} %get-tuple-element.223, f32[32,128,256]{2,1,0:T(8,128)} %fusion.60), kind=kCustom, calls=%fused_computation.4.clone.1 | custom fusion | flops 1048576 | bytes 12583040 | tf_op jit(solution)/shard_map/while/body/eval_jaxpr/scatter-add | solution.py:91
  471.5 10.0 %scatter_fusion.1 = f32[32,128,256]{2,1,0:T(8,128)} fusion(f32[32,128,256]{2,1,0:T(8,128)} %get-tuple-element.257, s32[32]{0:T(128)S(1)} %get-tuple-element.223, f32[32,128,256]{2,1,0:T(8,128)} %fusion.60), kind=kCustom, calls=%fused_computation.4.clone.1 | custom fusion | flops 1048576 | bytes 12583040 | tf_op jit(solution)/shard_map/while/body/eval_jaxpr/scatter-add | solution.py:91
  486.7 10.1 %scatter_fusion.1 = f32[32,128,256]{2,1,0:T(8,128)} fusion(f32[32,128,256]{2,1,0:T(8,128)} %get-tuple-element.257, s32[32]{0:T(128)S(1)} %get-tuple-element.223, f32[32,128,256]{2,1,0:T(8,128)} %fusion.60), kind=kCustom, calls=%fused_computation.4.clone.1 | custom fusion | flops 1048576 | bytes 12583040 | tf_op jit(solution)/shard_map/while/body/eval_jaxpr/scatter-add | solution.py:91
  502.0 9.9 %scatter_fusion.1 = f32[32,128,256]{2,1,0:T(8,128)} fusion(f32[32,128,256]{2,1,0:T(8,128)} %get-tuple-element.257, s32[32]{0:T(128)S(1)} %get-tuple-element.223, f32[32,128,256]{2,1,0:T(8,128)} %fusion.60), kind=kCustom, calls=%fused_computation.4.clone.1 | custom fusion | flops 1048576 | bytes 12583040 | tf_op jit(solution)/shard_map/while/body/eval_jaxpr/scatter-add | solution.py:91
  517.1 10.0 %scatter_fusion.1 = f32[32,128,256]{2,1,0:T(8,128)} fusion(f32[32,128,256]{2,1,0:T(8,128)} %get-tuple-element.257, s32[32]{0:T(128)S(1)} %get-tuple-element.223, f32[32,128,256]{2,1,0:T(8,128)} %fusion.60), kind=kCustom, calls=%fused_computation.4.clone.1 | custom fusion | flops 1048576 | bytes 12583040 | tf_op jit(solution)/shard_map/while/body/eval_jaxpr/scatter-add | solution.py:91
  532.2 9.9 %scatter_fusion.1 = f32[32,128,256]{2,1,0:T(8,128)} fusion(f32[32,128,256]{2,1,0:T(8,128)} %get-tuple-element.257, s32[32]{0:T(128)S(1)} %get-tuple-element.223, f32[32,128,256]{2,1,0:T(8,128)} %fusion.60), kind=kCustom, calls=%fused_computation.4.clone.1 | custom fusion | flops 1048576 | bytes 12583040 | tf_op jit(solution)/shard_map/while/body/eval_jaxpr/scatter-add | solution.py:91
  547.3 9.8 %scatter_fusion.1 = f32[32,128,256]{2,1,0:T(8,128)} fusion(f32[32,128,256]{2,1,0:T(8,128)} %get-tuple-element.257, s32[32]{0:T(128)S(1)} %get-tuple-element.223, f32[32,128,256]{2,1,0:T(8,128)} %fusion.60), kind=kCustom, calls=%fused_computation.4.clone.1 | custom fusion | flops 1048576 | bytes 12583040 | tf_op jit(solution)/shard_map/while/body/eval_jaxpr/scatter-add | solution.py:91
  557.7 40.9 %psum.46 = f32[256]{0:T(256)S(1)} all-reduce(f32[256]{0:T(256)S(1)} %copy-done.7), channel_id=1, replica_groups=mesh['nodes'=16,'cols'=8] {'nodes'}, use_global_device_ids=true, to_apply=%region_16.17 | all-reduce | flops 256 | bytes 2048 | tf_op jit(solution)/shard_map/psum | solution.py:9
  598.6 13.8 %psum.47 = f32[256]{0:T(256)} all-reduce(f32[256]{0:T(256)S(1)} %psum.46), channel_id=1, replica_groups=mesh['nodes'=16,'cols'=8] {'cols'}, use_global_device_ids=true, to_apply=%region_17.18 | all-reduce | flops 256 | bytes 2048 | tf_op jit(solution)/shard_map/psum | solution.py:10
  614.2 20.8 %reduce-scatter.5.cloned.1.call-done = f32[256,256]{1,0:T(8,128)} async-done(((f32[4096,256]{1,0:T(8,128)}), f32[256,256]{1,0:T(8,128)}) %reduce-scatter.5.cloned.1.call-update) | async-done | bytes 262160 | tf_op jit(solution)/shard_map/reduce_scatter | solution.py:99
  (230 shorter events, 185.9 us)
Async XLA Ops:
  7.2 267.5 %copy-start = (bf16[256,256]{1,0:T(8,128)(2,1)S(1)}, bf16[256,256]{1,0:T(8,128)(2,1)}, u32[]{:S(2)}) copy-start(bf16[256,256]{1,0:T(8,128)(2,1)} %param.17) | copy-start | bytes 393220
  7.2 50.7 %all-gather.3.cloned.1.call-start = ((), (), s32[]{:S(2)}) async-start(), calls=%async_computation.2 | async-start | bytes 2228224 | tf_op jit(solution)/shard_map/all_gather | solution.py:33
  7.9 266.8 %reduce-scatter.3.cloned.1.call-start = ((), (), s32[]{:S(2)}) async-start(), calls=%async_computation.3 | async-start | bytes 2359296 | tf_op jit(solution)/shard_map/reduce_scatter | solution.py:55
  240.2 1.4 copy-start.1
  240.2 2.0 copy-start.5
  240.2 2.0 copy-start.6
  240.3 1.4 copy-start.11
  240.3 2.6 copy-start.3
  240.3 2.6 copy-start.4
  240.3 34.4 %copy-start.9 = (bf16[256,256]{1,0:T(8,128)(2,1)S(1)}, bf16[256,256]{1,0:T(8,128)(2,1)}, u32[]{:S(2)}) copy-start(bf16[256,256]{1,0:T(8,128)(2,1)} %param.19) | copy-start | bytes 393220
  240.3 34.4 %copy-start.10 = (f32[256]{0:T(256)S(1)}, f32[256]{0:T(256)}, u32[]{:S(2)}) copy-start(f32[256]{0:T(256)} %param.18) | copy-start | bytes 3076
  241.6 122.0 %all-reduce.6.cloned.1.call-start = ((), (), s32[]{:S(2)}) async-start(), calls=%async_computation.6 | async-start | bytes 1048576 | tf_op jit(solution)/shard_map/psum | solution.py:9
  274.7 3.5 copy-start.8
  279.3 109.2 %all-gather.5.cloned.1.call-start = ((), (), s32[]{:S(2)}) async-start(), calls=%async_computation.4 | async-start | bytes 1179648 | tf_op jit(solution)/shard_map/all_gather | solution.py:83
  280.2 332.1 %all-reduce.8.cloned.1.call-start = ((), (), s32[]{:S(2)}) async-start(), calls=%async_computation.7 | async-start | bytes 1048576 | tf_op jit(solution)/shard_map/psum | solution.py:10
  363.6 271.4 %reduce-scatter.5.cloned.1.call-start = ((), (), s32[]{:S(2)}) async-start(), calls=%async_computation.5 | async-start | bytes 4456448 | tf_op jit(solution)/shard_map/reduce_scatter | solution.py:99
  388.5 2.4 copy-start.2
  557.1 0.7 copy-start.7
Sparse Core Ops, SparseCore 0:
  10.2 47.7 all-gather.2
  241.7 32.9 reduce-scatter.2
  279.4 84.1 all-reduce.5
  365.8 22.6 all-gather.4
  390.9 60.7 all-reduce.7
  557.2 77.6 reduce-scatter.4
